TPU v7x, 512 devices: a whole 4x4x16 slice. The times are simulated.
512 devices in a mesh: row: 16 (over z), col: 32 (over x, y, core).
Axes of the slice: x: 4, y: 4, z: 16, core: 2. Of those that a mesh axis runs over, the one named last changes fastest.
Arguments:
- gate_pre: bfloat16 [2048, 16384], P('row', 'col'), may hold values from -6 to 6
- up_pre: bfloat16 [2048, 16384], P('row', 'col'), may hold values from -6 to 6
- down_weight: bfloat16 [8192, 16384], P('row', 'col'), may hold values from -0.125 to 0.125
- block_mask: int32 [64, 128], P('row', 'col'), may hold values from 0 to 1, as said below
- cotangent: bfloat16 [2048, 8192], P('row', 'col'), may hold values from -6 to 6
Outputs:
- output: bfloat16 [2048, 8192], P('row', 'col')
- d_gate: bfloat16 [2048, 16384], P('row', 'col')
- d_up: bfloat16 [2048, 16384], P('row', 'col')
- d_down: bfloat16 [8192, 16384], P('row', 'col')
Inputs may be any that keep to these rules, and one draw needn't show every extreme that they name: `block_mask`: each device's tile of 4 x 4 blocks keeps between 4 and 12 blocks; in every draw some tile keeps exactly 12.
All inputs are finite; a program needn't handle non-finite values.
Results may differ from a plain program's by a relative error of at most 0.015.
Values may be sent and summed in bfloat16 or wider, within the bound.
A program may use at most 64 MiB of HBM per device.

v0:
```python
import jax
import jax.numpy as jnp
from jax import lax
from jax.sharding import PartitionSpec as P


def rounded_f32(values):
    return lax.optimization_barrier(values.astype(jnp.bfloat16)).astype(jnp.float32)


def body(gate_pre, up_pre, down_weight, block_mask, cotangent):
    tok_rows, ff_cols = gate_pre.shape
    d_rows = down_weight.shape[0]
    tile_r, tile_c = block_mask.shape
    block_size = d_rows // tile_r
    gate_wide = gate_pre.astype(jnp.float32)
    up_wide = up_pre.astype(jnp.float32)
    activated = jax.nn.silu(gate_wide)
    hidden = (activated * up_wide).astype(jnp.bfloat16)
    expand = jnp.repeat(jnp.repeat(block_mask, block_size, axis=0), block_size, axis=1)
    masked = jnp.where(expand > 0, down_weight, jnp.zeros_like(down_weight))
    cot_row = lax.all_gather(cotangent, "col", axis=1, tiled=True)
    cot_all = lax.all_to_all(cot_row, "row", split_axis=1, concat_axis=0, tiled=True)
    panel = lax.all_gather(masked, "row", axis=0, tiled=True)
    columns = lax.dot_general(
        hidden, panel, (((1,), (1,)), ((), ())), preferred_element_type=jnp.float32
    )
    y_partial = columns
    shards = panel.shape[0] // d_rows
    per_shard = jnp.einsum(
        "tnd,ndf->ntf",
        cot_row.reshape(tok_rows, shards, d_rows),
        panel.reshape(shards, d_rows, ff_cols),
        preferred_element_type=jnp.float32,
    )
    d_hidden = jnp.sum(rounded_f32(per_shard), axis=0)
    y_partial, d_hidden = (y_partial, d_hidden)
    y_summand = rounded_f32(y_partial)
    hidden_all = lax.all_gather(hidden, "row", axis=0, tiled=True)
    grad_full = lax.dot_general(
        cot_all, hidden_all, (((0,), (0,)), ((), ())), preferred_element_type=jnp.float32
    )
    output = lax.psum_scatter(
        y_summand.astype(jnp.bfloat16), "col", scatter_dimension=1, tiled=True
    )
    sigmoid_g = jax.nn.sigmoid(gate_wide)
    d_gate = (d_hidden * up_wide * sigmoid_g * (1.0 + gate_wide * (1.0 - sigmoid_g))).astype(
        jnp.bfloat16
    )
    d_up = (d_hidden * activated).astype(jnp.bfloat16)
    d_down = jnp.where(expand > 0, grad_full, jnp.zeros_like(grad_full)).astype(jnp.bfloat16)
    return (output, d_gate, d_up, d_down)


def solution(mesh):
    in_specs = (P("row", "col"), P("row", "col"), P("row", "col"), P("row", "col"), P("row", "col"))
    out_specs = (P("row", "col"), P("row", "col"), P("row", "col"), P("row", "col"))
    return jax.shard_map(body, mesh=mesh, in_specs=in_specs, out_specs=out_specs, check_vma=False)
```

profile of v0, /device:TPU:2, one launch (start us, length us, event | category | flops | bytes accessed | tf_op | source)
XLA Modules:
  0.0 470.4 jit_solution(9010206070040514916)
XLA Ops:
  7.2 0.0 all-gather.6.cloned.1.call-start
  7.2 1.6 copy.32
  8.9 0.0 all-gather.6.cloned.1.call-update
  8.9 0.0 all-gather.4.cloned.1.call-start
  8.9 0.7 broadcast_compare_fusion
  9.6 0.1 copy.29
  9.7 0.1 broadcast_bitcast_fusion
  9.8 1.3 copy.30
  11.1 0.8 bitcast_select_fusion.1
  11.9 0.0 all-gather.4.cloned.1.call-update
  12.0 0.1 copy.27
  12.1 0.1 copy.28
  12.2 62.5 %all-gather.6.cloned.1.call-done = bf16[128,8192]{0,1:T(8,128)(2,1)} async-done(((bf16[128,256]{0,1:T(8,128)(2,1)}), bf16[128,8192]{0,1:T(8,128)(2,1)}) %all-gather.6.cloned.1.call-update) | async-done | bytes 2097168 | tf_op jit(solution)/shard_map/all_gather | solution.py:22
  74.7 12.3 %all-to-all-start = ((bf16[128,16,512]{0,2,1:T(8,128)(2,1)}), bf16[128,16,512]{0,2,1:T(8,128)(2,1)S(1)}, u32[]{:S(2)}, u32[]{:S(2)}) async-start(bf16[128,16,512]{0,2,1:T(8,128)(2,1)} %bitcast.33), calls=%async_computation.1 | async-start | bytes 4194304 | tf_op jit(solution)/shard_map/all_to_all | solution.py:23
  87.0 0.0 all-gather.8.cloned.1.call-start
  87.1 179.0 %all-gather.4.cloned.1.call-done = bf16[8192,512]{0,1:T(8,128)(2,1)} async-done(((bf16[512,512]{0,1:T(8,128)(2,1)}), bf16[8192,512]{0,1:T(8,128)(2,1)}) %all-gather.4.cloned.1.call-update) | async-done | bytes 8388624 | tf_op jit(solution)/shard_map/all_gather | solution.py:24
  266.1 11.9 %copy.31 = bf16[8192,512]{1,0:T(8,128)(2,1)} copy(bf16[8192,512]{0,1:T(8,128)(2,1)} %all-gather.4.cloned.1.call-done) | data formatting | bytes 16777216 | tf_op jit(solution)/shard_map/all_gather | solution.py:24
  277.9 6.5 %convert_bitcast_fusion = bf16[16,128,512]{1,2,0:T(8,128)(2,1)S(1)} fusion(bf16[16,512,512]{2,1,0:T(8,128)(2,1)} %bitcast.30, bf16[128,16,512]{0,2,1:T(8,128)(2,1)} %bitcast.34), kind=kOutput, calls=%fused_computation.2 | convolution fusion | flops 1074790400 | bytes 12582912 | tf_op jit(solution)/shard_map/tnd,ndf->ntf/dot_general | solution.py:30
  284.4 0.3 convert_reduce_fusion
  284.7 0.8 multiply_convert_fusion
  285.6 0.0 all-gather.8.cloned.1.call-update
  285.6 0.0 reduce-scatter.2.cloned.1.call-start
  285.6 6.1 %convolution_convert_fusion = bf16[128,8192]{1,0:T(8,128)(2,1)} fusion(bf16[128,512]{0,1:T(8,128)(2,1)} %get-tuple-element.22, bf16[8192,512]{0,1:T(8,128)(2,1)} %all-gather.4.cloned.1.call-done), kind=kOutput, calls=%fused_computation | convolution fusion | flops 1074790400 | bytes 10616832 | tf_op jit(solution)/shard_map/dot_general | solution.py:25
  291.8 0.0 reduce-scatter.2.cloned.1.call-update
  291.8 0.0 all-to-all-done
  291.8 2.6 copy.35
  294.4 0.8 copy.36
  295.2 0.8 copy.37
  296.0 65.9 %all-gather.8.cloned.1.call-done = bf16[2048,512]{0,1:T(8,128)(2,1)} async-done(((bf16[128,512]{0,1:T(8,128)(2,1)}), bf16[2048,512]{0,1:T(8,128)(2,1)}) %all-gather.8.cloned.1.call-update) | async-done | bytes 2097168 | tf_op jit(solution)/shard_map/all_gather | solution.py:39
  361.9 3.5 fusion
  365.3 1.0 copy.38
  366.4 97.6 %reduce-scatter.2.cloned.1.call-done = bf16[128,256]{1,0:T(8,128)(2,1)} async-done(((bf16[128,8192]{1,0:T(8,128)(2,1)}), bf16[128,256]{1,0:T(8,128)(2,1)}) %reduce-scatter.2.cloned.1.call-update) | async-done | bytes 65552 | tf_op jit(solution)/shard_map/reduce_scatter | solution.py:43
  (5 shorter events, 0.0 us)
Async XLA Ops:
  7.2 4.8 %copy-start = (bf16[128,512]{1,0:T(8,128)(2,1)S(1)}, bf16[128,512]{1,0:T(8,128)(2,1)}, u32[]{:S(2)}) copy-start(bf16[128,512]{1,0:T(8,128)(2,1)} %param.5) | copy-start | bytes 393220
  7.2 4.9 %copy-start.1 = (bf16[128,512]{1,0:T(8,128)(2,1)S(1)}, bf16[128,512]{1,0:T(8,128)(2,1)}, u32[]{:S(2)}) copy-start(bf16[128,512]{1,0:T(8,128)(2,1)} %param.6) | copy-start | bytes 393220
  7.2 67.5 %all-gather.6.cloned.1.call-start = ((), (), s32[]{:S(2)}) async-start(), calls=%async_computation.4 | async-start | bytes 2162688 | tf_op jit(solution)/shard_map/all_gather | solution.py:22
  8.9 257.2 %all-gather.4.cloned.1.call-start = ((), (), s32[]{:S(2)}) async-start(), calls=%async_computation.2 | async-start | bytes 8912896 | tf_op jit(solution)/shard_map/all_gather | solution.py:24
  74.7 217.1 %all-to-all-start = ((bf16[128,16,512]{0,2,1:T(8,128)(2,1)}), bf16[128,16,512]{0,2,1:T(8,128)(2,1)S(1)}, u32[]{:S(2)}, u32[]{:S(2)}) async-start(bf16[128,16,512]{0,2,1:T(8,128)(2,1)} %bitcast.33), calls=%async_computation.1 | async-start | bytes 4194304 | tf_op jit(solution)/shard_map/all_to_all | solution.py:23
  87.0 274.9 %all-gather.8.cloned.1.call-start = ((), (), s32[]{:S(2)}) async-start(), calls=%async_computation.5 | async-start | bytes 2228224 | tf_op jit(solution)/shard_map/all_gather | solution.py:39
  285.6 178.3 %reduce-scatter.2.cloned.1.call-start = ((), (), s32[]{:S(2)}) async-start(), calls=%async_computation.3 | async-start | bytes 2162688 | tf_op jit(solution)/shard_map/reduce_scatter | solution.py:43
Sparse Core Ops, SparseCore 0:
  11.7 62.9 all-gather.5
  77.4 188.6 all-gather.3
  285.7 76.1 all-gather.7
  366.7 97.1 reduce-scatter.1
where the time goes:
time: 471 us; the launch traced here: 470 us
  waiting for transfers between devices  405 us (86%)
  local copies, waits for them, and re-layouts  20.3 us (4%)
  matrix products  16.1 us (3%)
  between operations  13.8 us (3%)
  starting transfers between devices  12.4 us (3%)
    all_gather x1, waiting for transfers between devices, body(): panel = lax.all_gather(masked, 'row', axis=0, tiled=True)  179 us
    reduce_scatter x1, waiting for transfers between devices, body(): lax.psum_scatter(y_summand.astype(jnp.bfloat16), 'col', scatter_dimension...  97.6 us
    all_gather x1, waiting for transfers between devices, body(): hidden_all = lax.all_gather(hidden, 'row', axis=0, tiled=True)  65.9 us
    all_gather x1, waiting for transfers between devices, body(): cot_row = lax.all_gather(cotangent, 'col', axis=1, tiled=True)  62.5 us
    all_to_all x1, starting transfers between devices, body(): lax.all_to_all(cot_row, 'row', split_axis=1, concat_axis=0, tiled=True)  12.3 us
    all_gather x1, local copies, waits for them, and re-layouts, body(): panel = lax.all_gather(masked, 'row', axis=0, tiled=True)  11.9 us
  transfers between devices with their start and end apart: 5, of which 4 were waited for; matrix products, arithmetic and copies ran while one was open for 8% of the time, Pallas kernels for 0%

commit v1 on v0

--- a/solution.py
+++ b/solution.py
@@ -19,7 +19,9 @@
     hidden = (activated * up_wide).astype(jnp.bfloat16)
     expand = jnp.repeat(jnp.repeat(block_mask, block_size, axis=0), block_size, axis=1)
     masked = jnp.where(expand > 0, down_weight, jnp.zeros_like(down_weight))
-    cot_row = lax.all_gather(cotangent, "col", axis=1, tiled=True)
+    cot_row = jnp.concatenate(
+        lax.all_to_all(jnp.stack([cotangent] * lax.axis_size("col")), "col", 0, 0), axis=1
+    )
     cot_all = lax.all_to_all(cot_row, "row", split_axis=1, concat_axis=0, tiled=True)
     panel = lax.all_gather(masked, "row", axis=0, tiled=True)
     columns = lax.dot_general(

time: 471 us -> 417 us (0.89)
  waiting for transfers between devices: 405 us -> 340 us
  starting transfers between devices: 12.4 us -> 23.1 us
    all_gather x1 -> x0, waiting for transfers between devices: 62.5 us -> none  [body(): cot_row = lax.all_gather(cotangent, 'col', axis=1, tiled=True)]
    all_gather x1, waiting for transfers between devices: 179 us -> 150 us  [body(): panel = lax.all_gather(masked, 'row', axis=0, tiled=True)]
    all_to_all x0 -> x1, waiting for transfers between devices: none -> 25.7 us  [body(): lax.all_to_all(jnp.stack([cotangent] * lax.axis_size('col')), 'col', 0, 0)]
    all_to_all x0 -> x1, starting transfers between devices: none -> 10.4 us  [body(): lax.all_to_all(jnp.stack([cotangent] * lax.axis_size('col')), 'col', 0, 0)]
  transfers between devices with their start and end apart: 5 -> 5, of which waited for: 4 -> 4; matrix products, arithmetic and copies ran while one was open for 8% -> 9% of each run, Pallas kernels for 0% -> 0%
where the time goes in v1:
time: 417 us; the launch traced here: 416 us
  waiting for transfers between devices  340 us (82%)
  starting transfers between devices  23.1 us (6%)
  local copies, waits for them, and re-layouts  20.7 us (5%)
  matrix products  16.1 us (4%)
  between operations  13.8 us (3%)
    all_gather x1, waiting for transfers between devices, body(): panel = lax.all_gather(masked, 'row', axis=0, tiled=True)  150 us
    reduce_scatter x1, waiting for transfers between devices, body(): lax.psum_scatter(y_summand.astype(jnp.bfloat16), 'col', scatter_dimension...  97.7 us
    all_gather x1, waiting for transfers between devices, body(): hidden_all = lax.all_gather(hidden, 'row', axis=0, tiled=True)  67 us
    all_to_all x1, waiting for transfers between devices, body(): lax.all_to_all(jnp.stack([cotangent] * lax.axis_size('col')), 'col', 0, 0)  25.7 us
    all_to_all x1, starting transfers between devices, body(): lax.all_to_all(cot_row, 'row', split_axis=1, concat_axis=0, tiled=True)  12.6 us
    all_gather x1, local copies, waits for them, and re-layouts, body(): panel = lax.all_gather(masked, 'row', axis=0, tiled=True)  11.9 us
    all_to_all x1, starting transfers between devices, body(): lax.all_to_all(jnp.stack([cotangent] * lax.axis_size('col')), 'col', 0, 0)  10.4 us
  transfers between devices with their start and end apart: 5, of which 4 were waited for; matrix products, arithmetic and copies ran while one was open for 9% of the time, Pallas kernels for 0%

profile of v1, /device:TPU:2, one launch (start us, length us, event | category | flops | bytes accessed | tf_op | source)
XLA Modules:
  0.0 416.4 jit_solution(968516433331875145)
XLA Ops:
  7.2 0.0 all-gather.3.cloned.1.call-start
  7.2 0.7 broadcast_compare_fusion
  7.9 0.1 copy.29
  8.0 0.1 broadcast_bitcast_fusion
  8.1 1.3 copy.30
  9.4 0.8 bitcast_select_fusion.1
  10.2 0.0 all-gather.3.cloned.1.call-update
  10.2 0.1 copy.32
  10.4 1.9 stack.2
  12.2 10.4 %all-to-all-start = ((bf16[32,128,256]{1,2,0:T(8,128)(2,1)}), bf16[32,128,256]{1,2,0:T(8,128)(2,1)}, u32[]{:S(2)}, u32[]{:S(2)}) async-start(bf16[32,128,256]{1,2,0:T(8,128)(2,1)} %stack.2), calls=%async_computation.1 | async-start | bytes 4194304 | tf_op jit(solution)/shard_map/all_to_all | solution.py:23
  22.6 0.1 copy.27
  22.8 0.1 copy.28
  22.9 25.7 %all-to-all-done = bf16[32,128,256]{1,2,0:T(8,128)(2,1)} async-done(((bf16[32,128,256]{1,2,0:T(8,128)(2,1)}), bf16[32,128,256]{1,2,0:T(8,128)(2,1)}, u32[]{:S(2)}, u32[]{:S(2)}) %all-to-all-start) | async-done | bytes 2097184 | tf_op jit(solution)/shard_map/all_to_all | solution.py:23
  48.6 12.6 %all-to-all-start.1 = ((bf16[128,16,512]{0,2,1:T(8,128)(2,1)}), bf16[128,16,512]{0,2,1:T(8,128)(2,1)S(1)}, u32[]{:S(2)}, u32[]{:S(2)}) async-start(bf16[128,16,512]{0,2,1:T(8,128)(2,1)} %bitcast.3), calls=%async_computation.2 | async-start | bytes 4194304 | tf_op jit(solution)/shard_map/all_to_all | solution.py:25
  61.2 0.0 all-gather.5.cloned.1.call-start
  61.2 149.7 %all-gather.3.cloned.1.call-done = bf16[8192,512]{0,1:T(8,128)(2,1)} async-done(((bf16[512,512]{0,1:T(8,128)(2,1)}), bf16[8192,512]{0,1:T(8,128)(2,1)}) %all-gather.3.cloned.1.call-update) | async-done | bytes 8388624 | tf_op jit(solution)/shard_map/all_gather | solution.py:26
  210.9 11.9 %copy.31 = bf16[8192,512]{1,0:T(8,128)(2,1)} copy(bf16[8192,512]{0,1:T(8,128)(2,1)} %all-gather.3.cloned.1.call-done) | data formatting | bytes 16777216 | tf_op jit(solution)/shard_map/all_gather | solution.py:26
  222.8 6.5 %convert_bitcast_fusion = bf16[16,128,512]{1,2,0:T(8,128)(2,1)S(1)} fusion(bf16[16,512,512]{2,1,0:T(8,128)(2,1)} %bitcast.32, bf16[128,16,512]{0,2,1:T(8,128)(2,1)} %bitcast.3), kind=kOutput, calls=%fused_computation.2 | convolution fusion | flops 1074790400 | bytes 12582912 | tf_op jit(solution)/shard_map/tnd,ndf->ntf/dot_general | solution.py:32
  229.3 0.3 convert_reduce_fusion
  229.6 0.8 multiply_convert_fusion
  230.4 0.0 all-gather.5.cloned.1.call-update
  230.4 0.0 reduce-scatter.2.cloned.1.call-start
  230.5 6.1 %convolution_convert_fusion = bf16[128,8192]{1,0:T(8,128)(2,1)} fusion(bf16[128,512]{0,1:T(8,128)(2,1)} %get-tuple-element.22, bf16[8192,512]{0,1:T(8,128)(2,1)} %all-gather.3.cloned.1.call-done), kind=kOutput, calls=%fused_computation | convolution fusion | flops 1074790400 | bytes 10616832 | tf_op jit(solution)/shard_map/dot_general | solution.py:27
  236.6 0.0 reduce-scatter.2.cloned.1.call-update
  236.6 0.0 all-to-all-done.1
  236.6 2.6 copy.35
  239.2 0.8 copy.36
  240.0 0.8 copy.37
  240.8 67.0 %all-gather.5.cloned.1.call-done = bf16[2048,512]{0,1:T(8,128)(2,1)} async-done(((bf16[128,512]{0,1:T(8,128)(2,1)}), bf16[2048,512]{0,1:T(8,128)(2,1)}) %all-gather.5.cloned.1.call-update) | async-done | bytes 2097168 | tf_op jit(solution)/shard_map/all_gather | solution.py:41
  307.8 3.5 fusion
  311.2 1.0 copy.38
  312.2 97.7 %reduce-scatter.2.cloned.1.call-done = bf16[128,256]{1,0:T(8,128)(2,1)} async-done(((bf16[128,8192]{1,0:T(8,128)(2,1)}), bf16[128,256]{1,0:T(8,128)(2,1)}) %reduce-scatter.2.cloned.1.call-update) | async-done | bytes 65552 | tf_op jit(solution)/shard_map/reduce_scatter | solution.py:45
  (7 shorter events, 0.0 us)
Async XLA Ops:
  7.2 3.1 copy-start.2
  7.2 203.7 %all-gather.3.cloned.1.call-start = ((), (), s32[]{:S(2)}) async-start(), calls=%async_computation.3 | async-start | bytes 8912896 | tf_op jit(solution)/shard_map/all_gather | solution.py:26
  12.2 10.4 %copy-start = (bf16[128,512]{1,0:T(8,128)(2,1)S(1)}, bf16[128,512]{1,0:T(8,128)(2,1)}, u32[]{:S(2)}) copy-start(bf16[128,512]{1,0:T(8,128)(2,1)} %param.5) | copy-start | bytes 393220
  12.2 10.5 %copy-start.1 = (bf16[128,512]{1,0:T(8,128)(2,1)S(1)}, bf16[128,512]{1,0:T(8,128)(2,1)}, u32[]{:S(2)}) copy-start(bf16[128,512]{1,0:T(8,128)(2,1)} %param.6) | copy-start | bytes 393220
  12.2 36.4 %all-to-all-start = ((bf16[32,128,256]{1,2,0:T(8,128)(2,1)}), bf16[32,128,256]{1,2,0:T(8,128)(2,1)}, u32[]{:S(2)}, u32[]{:S(2)}) async-start(bf16[32,128,256]{1,2,0:T(8,128)(2,1)} %stack.2), calls=%async_computation.1 | async-start | bytes 4194304 | tf_op jit(solution)/shard_map/all_to_all | solution.py:23
  48.6 188.0 %all-to-all-start.1 = ((bf16[128,16,512]{0,2,1:T(8,128)(2,1)}), bf16[128,16,512]{0,2,1:T(8,128)(2,1)S(1)}, u32[]{:S(2)}, u32[]{:S(2)}) async-start(bf16[128,16,512]{0,2,1:T(8,128)(2,1)} %bitcast.3), calls=%async_computation.2 | async-start | bytes 4194304 | tf_op jit(solution)/shard_map/all_to_all | solution.py:25
  61.2 246.6 %all-gather.5.cloned.1.call-start = ((), (), s32[]{:S(2)}) async-start(), calls=%async_computation.5 | async-start | bytes 2228224 | tf_op jit(solution)/shard_map/all_gather | solution.py:41
  230.4 179.5 %reduce-scatter.2.cloned.1.call-start = ((), (), s32[]{:S(2)}) async-start(), calls=%async_computation.4 | async-start | bytes 2162688 | tf_op jit(solution)/shard_map/reduce_scatter | solution.py:45
Sparse Core Ops, SparseCore 0:
  10.6 200.2 all-gather.2
  230.5 77.1 all-gather.4
  312.8 97.1 reduce-scatter.1
